TPU v7x, 1024 devices: a whole 4x4x32 slice. The times are simulated.
1024 devices in a mesh: seq: 32 (over z), tp: 8 (over y, core), dp: 4 (over x).
Axes of the slice: x: 4, y: 4, z: 32, core: 2. Of those that a mesh axis runs over, the one named last changes fastest.
Arguments:
- queries: bfloat16 [4, 4096, 8192], P('dp', 'seq', 'tp'), may hold values from -96 to 96
- images: bfloat16 [4, 32, 128, 8192], P('dp', 'seq', None, 'tp'), may hold values from -6 to 6
- kv_weight: bfloat16 [8192, 2048], P(None, 'tp'), may hold values from -0.0625 to 0.0625
- gate: float32 [1], replicated, may hold values from 0.3 to 1.5
- cotangent: bfloat16 [4, 4096, 8192], P('dp', 'seq', 'tp'), may hold values from -6 to 6
- span_first: int32 [4, 32], P('dp', 'seq'), may hold values from 0 to 30, as said below
- span_last: int32 [4, 32], P('dp', 'seq'), may hold values from 0 to 31, as said below
Outputs:
- attended: bfloat16 [4, 4096, 8192], P('dp', 'seq', 'tp')
- query_grad: bfloat16 [4, 4096, 8192], P('dp', 'seq', 'tp')
- weight_gradient: float32 [8192, 2048], P('seq', 'tp')
Inputs may be any that keep to these rules, and one draw needn't show every extreme that they name: Text block b attends images span_first to span_last of its group, with b - 3 <= span_first <= span_last <= b; the last block of every group attends 4 images, and where 4 > 2 the block before it attends only its own image. `span_last`: see span_first.
All inputs are finite; a program needn't handle non-finite values.
Results may differ from a plain program's by a relative error of at most 0.03.
Values may be sent and summed in bfloat16 or wider, within the bound.
A program may use at most 32 MiB of HBM per device.

v0:
```python
import jax
import jax.numpy as jnp
from jax import lax
from jax.sharding import PartitionSpec as P

QUERY_HEADS = 64
VALUE_HEADS = 8
HEAD_SIZE = 128


def shifted(value, axis, steps):
    count = lax.axis_size(axis)
    first, last = (max(0, -steps), min(count, count - steps))
    return lax.ppermute(value, axis, [(source, source + steps) for source in range(first, last)])


def attend(query_rows, key_rows, value_rows, is_live, gate_tanh, cotangent_rows):
    scale = HEAD_SIZE ** (-0.5)
    scores = (
        jnp.einsum("tkgd,wpkd->kgtwp", query_rows, key_rows, preferred_element_type=jnp.float32)
        * scale
    )
    scores = jnp.where(is_live[None, None, None, :, None], scores, -jnp.inf)
    row_max = jnp.max(scores, axis=(3, 4), keepdims=True)
    exponent = jnp.exp(scores - row_max)
    attn_prob = exponent / jnp.sum(exponent, axis=(3, 4), keepdims=True)
    prob_low = attn_prob.astype(jnp.bfloat16)
    context = jnp.einsum(
        "kgtwp,wpkd->tkgd", prob_low, value_rows, preferred_element_type=jnp.float32
    )
    attended_rows = (gate_tanh * context).astype(jnp.bfloat16)
    d_context = (gate_tanh * cotangent_rows.astype(jnp.float32)).astype(jnp.bfloat16)
    row_delta = jnp.transpose(jnp.sum(d_context.astype(jnp.float32) * context, axis=-1), (1, 2, 0))
    d_probs = jnp.einsum(
        "tkgd,wpkd->kgtwp", d_context, value_rows, preferred_element_type=jnp.float32
    )
    d_scores = (attn_prob * (d_probs - row_delta[..., None, None]) * scale).astype(jnp.bfloat16)
    grad_query = jnp.einsum(
        "kgtwp,wpkd->tkgd", d_scores, key_rows, preferred_element_type=jnp.float32
    ).astype(jnp.bfloat16)
    grad_keys = jnp.einsum(
        "kgtwp,tkgd->wpkd", d_scores, query_rows, preferred_element_type=jnp.float32
    )
    grad_values = jnp.einsum(
        "kgtwp,tkgd->wpkd", prob_low, d_context, preferred_element_type=jnp.float32
    )
    return (attended_rows, grad_query, grad_keys, grad_values)


def local(queries, images, kv_weight, gate, cotangent, span_first, span_last):
    features = images[0, 0]
    patches = features.shape[0]
    key_cols = kv_weight.shape[1]
    key_heads = key_cols // (2 * HEAD_SIZE)
    size_of_group = QUERY_HEADS // VALUE_HEADS
    block_rows = queries.shape[1]
    reach_count = min(4, lax.axis_size("seq") // 2)
    gate_tanh = jnp.tanh(gate[0])
    all_features = lax.all_gather(features, "tp", axis=1, tiled=True)
    key_value_pairs = jnp.dot(all_features, kv_weight, preferred_element_type=jnp.float32)
    key_value_pairs = key_value_pairs.astype(jnp.bfloat16)
    by_offset = [key_value_pairs]
    for offset in range(1, reach_count):
        by_offset.append(shifted(key_value_pairs, "seq", offset))
    window = jnp.stack(by_offset[::-1], 0).reshape(reach_count, patches, key_heads, 2, HEAD_SIZE)
    position = lax.axis_index("seq")
    image_index = position - reach_count + 1 + jnp.arange(reach_count, dtype=jnp.int32)
    is_live = (image_index >= span_first[0, 0]) & (image_index <= span_last[0, 0])
    query_rows = queries[0].reshape(block_rows, key_heads, size_of_group, HEAD_SIZE)
    cotangent_rows = cotangent[0].reshape(block_rows, key_heads, size_of_group, HEAD_SIZE)
    attended_rows, grad_query, grad_keys, grad_values = attend(
        query_rows, window[:, :, :, 0], window[:, :, :, 1], is_live, gate_tanh, cotangent_rows
    )
    grad_parts = jnp.stack([grad_keys, grad_values], 3).reshape(reach_count, patches, key_cols)
    kv_grad = grad_parts[reach_count - 1]
    for offset in range(1, reach_count):
        kv_grad = kv_grad + shifted(grad_parts[reach_count - 1 - offset], "seq", -offset)
    key_value_gradient_bf = kv_grad.astype(jnp.bfloat16)
    local_grad = lax.dot_general(
        all_features,
        key_value_gradient_bf,
        (((0,), (0,)), ((), ())),
        preferred_element_type=jnp.float32,
    )
    group_share = lax.psum_scatter(
        local_grad.astype(jnp.bfloat16), "seq", scatter_dimension=0, tiled=True
    ).astype(jnp.float32)
    weight_gradient = lax.psum(group_share, "dp")
    return (
        attended_rows.reshape(1, block_rows, -1),
        grad_query.reshape(1, block_rows, -1),
        weight_gradient,
    )


def solution(mesh):
    return jax.shard_map(
        local,
        mesh=mesh,
        in_specs=(
            P("dp", "seq", "tp"),
            P("dp", "seq", None, "tp"),
            P(None, "tp"),
            P(),
            P("dp", "seq", "tp"),
            P("dp", "seq"),
            P("dp", "seq"),
        ),
        out_specs=(P("dp", "seq", "tp"), P("dp", "seq", "tp"), P("seq", "tp")),
        check_vma=False,
    )
```

profile of v0, /device:TPU:24, one launch (start us, length us, event | category | flops | bytes accessed | tf_op | source)
XLA Modules:
  0.0 284.6 jit_solution(6506928854060318705)
XLA Ops:
  7.2 0.7 all-gather.3.cloned.1.call-update
  8.6 1.0 fusion.23
  9.7 1.0 copy.18
  12.1 0.8 copy.48
  12.8 0.9 copy.22
  13.7 46.8 %all-gather.3.cloned.1.call-done = bf16[1,1,128,8192]{3,2,1,0:T(8,128)(2,1)} async-done(((bf16[1,1,128,1024]{3,2,1,0:T(8,128)(2,1)}), bf16[1,1,128,8192]{3,2,1,0:T(8,128)(2,1)}) %all-gather.3.cloned.1.call-update) | async-done | bytes 2097168 | tf_op jit(solution)/shard_map/all_gather | solution.py:59
  60.5 3.5 %fusion.12 = bf16[128,256]{1,0:T(8,128)(2,1)S(1)} fusion(bf16[8192,256]{1,0:T(8,128)(2,1)} %param.9, bf16[1,1,128,8192]{3,2,1,0:T(8,128)(2,1)} %all-gather.3.cloned.1.call-done), kind=kOutput, calls=%fused_computation.21 | convolution fusion | flops 536903680 | bytes 6356992 | tf_op jit(solution)/shard_map/dot_general | solution.py:60
  64.1 4.8 %collective-permute-start = (bf16[128,256]{1,0:T(8,128)(2,1)S(1)}, bf16[128,256]{1,0:T(8,128)(2,1)S(1)}, u32[]{:S(2)}, u32[]{:S(2)}) collective-permute-start(bf16[128,256]{1,0:T(8,128)(2,1)S(1)} %fusion.12), channel_id=1, source_target_pairs={{0,96},{32,128},{64,160},{96,192},{128,224},{160,256},{192,288},{2... | collective-permute-start | bytes 196616 | tf_op jit(solution)/shard_map/ppermute | solution.py:14
  68.9 5.7 %collective-permute-start.1 = (bf16[128,256]{1,0:T(8,128)(2,1)S(1)}, bf16[128,256]{1,0:T(8,128)(2,1)S(1)}, u32[]{:S(2)}, u32[]{:S(2)}) collective-permute-start(bf16[128,256]{1,0:T(8,128)(2,1)S(1)} %fusion.12), channel_id=1, source_target_pairs={{0,64},{32,96},{64,128},{96,160},{128,192},{160,224},{192,256},{22... | collective-permute-start | bytes 196616 | tf_op jit(solution)/shard_map/ppermute | solution.py:14
  74.6 3.5 %collective-permute-start.2 = (bf16[128,256]{1,0:T(8,128)(2,1)S(1)}, bf16[128,256]{1,0:T(8,128)(2,1)S(1)}, u32[]{:S(2)}, u32[]{:S(2)}) collective-permute-start(bf16[128,256]{1,0:T(8,128)(2,1)S(1)} %fusion.12), channel_id=1, source_target_pairs={{0,32},{32,64},{64,96},{96,128},{128,160},{160,192},{192,224},{224... | collective-permute-start | bytes 196616 | tf_op jit(solution)/shard_map/ppermute | solution.py:14
  78.2 1.7 collective-permute-done.2
  81.8 1.5 copy.39
  83.2 1.5 multiply_reduce_fusion
  84.7 1.9 fusion.10
  87.6 1.3 collective-permute-start.5
  88.9 1.3 collective-permute-start.4
  90.2 1.3 collective-permute-start.3
  91.5 12.4 %collective-permute-done.5 = f32[128,256]{0,1:T(8,128)S(1)} collective-permute-done((f32[128,256]{0,1:T(8,128)S(1)}, f32[128,256]{0,1:T(8,128)S(1)}, u32[]{:S(2)}, u32[]{:S(2)}) %collective-permute-start.5) | collective-permute-done | bytes 131104 | tf_op jit(solution)/shard_map/ppermute | solution.py:14
  104.3 3.2 %fusion = bf16[8192,256]{0,1:T(8,128)(2,1)} fusion(bf16[128,256]{0,1:T(8,128)(2,1)S(1)} %fusion.29, bf16[1,1,128,8192]{3,2,1,0:T(8,128)(2,1)S(1)} %copy-done), kind=kOutput, calls=%fused_computation.1 | convolution fusion | flops 538968064 | bytes 6356992 | tf_op jit(solution)/shard_map/dot_general | solution.py:79
  107.5 0.9 copy.25
  108.8 0.9 copy.26
  109.6 146.8 %reduce-scatter.2.cloned.1.call-done = bf16[256,256]{0,1:T(8,128)(2,1)} async-done(((bf16[8192,256]{0,1:T(8,128)(2,1)}), bf16[256,256]{0,1:T(8,128)(2,1)}) %reduce-scatter.2.cloned.1.call-update) | async-done | bytes 131088 | tf_op jit(solution)/shard_map/reduce_scatter | solution.py:85
  256.4 20.4 %all-reduce.1 = f32[256,256]{0,1:T(8,128)S(1)} all-reduce(bf16[256,256]{0,1:T(8,128)(2,1)} %reduce-scatter.2.cloned.1.call-done), channel_id=1, replica_groups=mesh['seq'=32,'tp'=8,'dp'=4] {'dp'}, use_global_device_ids=true, to_apply=%region_4.5 | all-reduce | flops 65536 | bytes 393216 | tf_op jit(solution)/shard_map/psum | solution.py:88
  276.9 0.8 copy.27
  (39 shorter events, 3.7 us)
Async XLA Ops:
  7.2 4.8 %copy-start.6 = (bf16[1,128,1024]{2,1,0:T(8,128)(2,1)S(1)}, bf16[1,128,1024]{2,1,0:T(8,128)(2,1)}, u32[]{:S(2)}) copy-start(bf16[1,128,1024]{2,1,0:T(8,128)(2,1)} %param.7) | copy-start | bytes 786436
  7.2 53.4 %all-gather.3.cloned.1.call-start = ((), (), s32[]{:S(2)}) async-start(), calls=%async_computation.2 | async-start | bytes 2359296 | tf_op jit(solution)/shard_map/all_gather | solution.py:59
  7.9 248.5 %reduce-scatter.2.cloned.1.call-start = ((), (), s32[]{:S(2)}) async-start(), calls=%async_computation.1 | async-start | bytes 4325376 | tf_op jit(solution)/shard_map/reduce_scatter | solution.py:85
  64.1 14.0 %collective-permute-start = (bf16[128,256]{1,0:T(8,128)(2,1)S(1)}, bf16[128,256]{1,0:T(8,128)(2,1)S(1)}, u32[]{:S(2)}, u32[]{:S(2)}) collective-permute-start(bf16[128,256]{1,0:T(8,128)(2,1)S(1)} %fusion.12), channel_id=1, source_target_pairs={{0,96},{32,128},{64,160},{96,192},{128,224},{160,256},{192,288},{2... | collective-permute-start | bytes 196616 | tf_op jit(solution)/shard_map/ppermute | solution.py:14
  68.9 9.2 %collective-permute-start.1 = (bf16[128,256]{1,0:T(8,128)(2,1)S(1)}, bf16[128,256]{1,0:T(8,128)(2,1)S(1)}, u32[]{:S(2)}, u32[]{:S(2)}) collective-permute-start(bf16[128,256]{1,0:T(8,128)(2,1)S(1)} %fusion.12), channel_id=1, source_target_pairs={{0,64},{32,96},{64,128},{96,160},{128,192},{160,224},{192,256},{22... | collective-permute-start | bytes 196616 | tf_op jit(solution)/shard_map/ppermute | solution.py:14
  74.6 5.4 %collective-permute-start.2 = (bf16[128,256]{1,0:T(8,128)(2,1)S(1)}, bf16[128,256]{1,0:T(8,128)(2,1)S(1)}, u32[]{:S(2)}, u32[]{:S(2)}) collective-permute-start(bf16[128,256]{1,0:T(8,128)(2,1)S(1)} %fusion.12), channel_id=1, source_target_pairs={{0,32},{32,64},{64,96},{96,128},{128,160},{160,192},{192,224},{224... | collective-permute-start | bytes 196616 | tf_op jit(solution)/shard_map/ppermute | solution.py:14
  80.0 0.7 copy-start.4
  84.7 2.0 copy-start.1
  84.7 2.0 copy-start.3
  84.7 2.3 copy-start.2
  86.7 17.6 %copy-start = (bf16[1,1,128,8192]{3,2,1,0:T(8,128)(2,1)S(1)}, bf16[1,1,128,8192]{3,2,1,0:T(8,128)(2,1)}, u32[]{:S(2)}) copy-start(bf16[1,1,128,8192]{3,2,1,0:T(8,128)(2,1)} %all-gather.3.cloned.1.call-done) | copy-start | bytes 6291460
  87.6 16.3 %collective-permute-start.5 = (f32[128,256]{0,1:T(8,128)S(1)}, f32[128,256]{0,1:T(8,128)S(1)}, u32[]{:S(2)}, u32[]{:S(2)}) collective-permute-start(f32[128,256]{0,1:T(8,128)S(1)} %bitcast.177), channel_id=1, source_target_pairs={{96,0},{128,32},{160,64},{192,96},{224,128},{256,160},{288,192},{3... | collective-permute-start | bytes 393224 | tf_op jit(solution)/shard_map/ppermute | solution.py:14
  88.9 15.4 %collective-permute-start.4 = (f32[128,256]{0,1:T(8,128)S(1)}, f32[128,256]{0,1:T(8,128)S(1)}, u32[]{:S(2)}, u32[]{:S(2)}) collective-permute-start(f32[128,256]{0,1:T(8,128)S(1)} %bitcast.176), channel_id=1, source_target_pairs={{64,0},{96,32},{128,64},{160,96},{192,128},{224,160},{256,192},{28... | collective-permute-start | bytes 393224 | tf_op jit(solution)/shard_map/ppermute | solution.py:14
  90.2 14.1 %collective-permute-start.3 = (f32[128,256]{0,1:T(8,128)S(1)}, f32[128,256]{0,1:T(8,128)S(1)}, u32[]{:S(2)}, u32[]{:S(2)}) collective-permute-start(f32[128,256]{0,1:T(8,128)S(1)} %bitcast.175), channel_id=1, source_target_pairs={{32,0},{64,32},{96,64},{128,96},{160,128},{192,160},{224,192},{256... | collective-permute-start | bytes 393224 | tf_op jit(solution)/shard_map/ppermute | solution.py:14
  107.5 0.9 copy-start.5
Sparse Core Ops, SparseCore 0:
  10.7 49.8 all-gather.2
  107.6 148.7 reduce-scatter.1
where the time goes:
time: 285 us
  waiting for transfers between devices  209 us (73%)
  blocking collectives  20.4 us (7%)
  starting transfers between devices  17.9 us (6%)
  between operations  16.3 us (6%)
  matrix products  11.7 us (4%)
  local copies, waits for them, and re-layouts  7.21 us (3%)
    reduce_scatter x1, waiting for transfers between devices, local(): lax.psum_scatter(local_grad.astype(jnp.bfloat16), 'seq', scatter_dimensio...  147 us
    all_gather x1, waiting for transfers between devices, local(): all_features = lax.all_gather(features, 'tp', axis=1, tiled=True)  46.8 us
    psum x1, blocking collectives, local(): weight_gradient = lax.psum(group_share, 'dp')  20.4 us
    ppermute x6, starting transfers between devices, shifted(): lax.ppermute(value, axis, [(source, source + steps) for source in range(f...  17.8 us
    ppermute x6, waiting for transfers between devices, shifted(): lax.ppermute(value, axis, [(source, source + steps) for source in range(f...  14.5 us
  transfers between devices with their start and end apart: 8, of which 5 were waited for; matrix products, arithmetic and copies ran while one was open for 2% of the time, Pallas kernels for 0%

commit v1 on v0

v1 whole, which is shorter than its diff:
```python
import functools

import jax
import jax.numpy as jnp
from jax import lax
from jax.experimental import pallas as pl
from jax.experimental.pallas import tpu as pltpu
from jax.sharding import PartitionSpec as P

HEADS = 8
HEAD_SIZE = 128
TOKENS = 128
PATCHES = 128
REACH = 4
TP = 8
DP = 4
SHARD = 1024
HALF = SHARD // 2
KVC = 2 * HEAD_SIZE
SCALE = HEAD_SIZE ** (-0.5)
GATHER_COPIES = 14
PARTS = 2

BF16 = jnp.bfloat16
F32 = jnp.float32


def remote(src, dst, send_sem, recv_sem, **where):
    return pltpu.make_async_remote_copy(
        src_ref=src,
        dst_ref=dst,
        send_sem=send_sem,
        recv_sem=recv_sem,
        device_id=where,
        device_id_type=pl.DeviceIdType.MESH,
    )


class RowGather:
    def __init__(self, own, slot, send_sems, recv_sems):
        tp = lax.axis_index("tp")
        self.tp = tp
        self.right, self.left = lax.rem(tp + 2, TP), lax.rem(tp + TP - 2, TP)
        self.opposite = lax.rem(tp + 4, TP)
        self.sibling = tp + 1 - 2 * lax.rem(tp, 2)
        self.own, self.slot = own, slot
        self.send_sems, self.recv_sems = send_sems, recv_sems
        self.started = []

    def _copy(self, index, src, dst, target):
        return remote(src, dst, self.send_sems.at[index], self.recv_sems.at[index], tp=target)

    def _start(self, index, src, owner, half, target):
        copy = self._copy(index, src, self.slot(owner, half), target)
        copy.start()
        self.started.append(copy)

    def _arrived(self, index, owner, half):
        ref = self.slot(owner, half)
        self._copy(index, ref, ref, self.right).wait_recv()

    def send_own(self):
        for half in (0, 1):
            self._start(half, self.own(half), self.tp, half, self.right)
            self._start(3 - half, self.own(1 - half), self.tp, 1 - half, self.left)
        for half in (0, 1):
            self._start(6 + half, self.own(half), self.tp, half, self.sibling)

    def sibling_own(self, half):
        self._arrived(6 + half, self.sibling, half)
        return self.sibling, half

    def from_left(self, half):
        self._arrived(half, self.left, half)
        ref = self.slot(self.left, half)
        if half == 0:
            self._start(4, ref, self.left, half, self.right)
        self._start(8 + half, ref, self.left, half, self.sibling)
        return self.left, half

    def from_right(self, half):
        self._arrived(2 + half, self.right, half)
        ref = self.slot(self.right, half)
        if half == 1:
            self._start(5, ref, self.right, half, self.left)
        self._start(10 + half, ref, self.right, half, self.sibling)
        return self.right, half

    def from_opposite(self, half):
        self._arrived(4 + half, self.opposite, half)
        self._start(12 + half, self.slot(self.opposite, half), self.opposite, half, self.sibling)
        return self.opposite, half

    def sibling_other(self, which, half):
        owner = lax.rem(self.sibling + (TP - 2, 2, 4)[which], TP)
        self._arrived(8 + 2 * which + half, owner, half)
        return owner, half

    def finish(self):
        for copy in self.started:
            copy.wait_send()


def kernel(
    nz,
    queries,
    features,
    kv_weight,
    gate,
    cotangent,
    span_first,
    span_last,
    attended_out,
    query_grad_out,
    weight_out,
    q_buf,
    cot_buf,
    w_buf,
    gathered,
    proj,
    transposed,
    columns,
    q_t,
    dc_buf,
    dc_t,
    keys,
    values,
    scores,
    d_probs,
    p_buf,
    ds_buf,
    att_buf,
    dq_buf,
    part,
    chain_out,
    chain_in,
    dkv,
    term,
    ring_out,
    ring_in,
    quarter,
    local_sems,
    feat_send,
    feat_recv,
    col_send,
    col_recv,
    cross_send,
    cross_recv,
    kv_send,
    kv_recv,
    chain_send,
    chain_recv,
    dkv_send,
    dkv_recv,
    ring_send,
    ring_recv,
    last_send,
    last_recv,
):
    z, tp, dp = lax.axis_index("seq"), lax.axis_index("tp"), lax.axis_index("dp")
    z_next, z_prev = lax.rem(z + 1, nz), lax.rem(z + nz - 1, nz)

    w_copies = []
    in_q = pltpu.make_async_copy(queries.at[0], q_buf, local_sems.at[0])
    in_cot = pltpu.make_async_copy(cotangent.at[0], cot_buf, local_sems.at[1])
    in_w = pltpu.make_async_copy(kv_weight, w_buf, local_sems.at[2])
    in_q.start()
    in_cot.start()
    in_w.start()

    gather = RowGather(
        lambda half: features.at[0, 0, :, pl.ds(half * HALF, HALF)],
        lambda owner, half: gathered.at[owner, :, pl.ds(half * HALF, HALF)],
        feat_send,
        feat_recv,
    )
    barrier = pltpu.get_barrier_semaphore()
    mesh_id = pl.DeviceIdType.MESH
    for other in (gather.right, gather.left, gather.sibling):
        pl.semaphore_signal(barrier, inc=1, device_id={"tp": other}, device_id_type=mesh_id)
    for steps in range(1, DP):
        other = lax.rem(dp + steps, DP)
        pl.semaphore_signal(barrier, inc=1, device_id={"dp": other}, device_id_type=mesh_id)
    for other in (z_next, z_prev):
        pl.semaphore_signal(barrier, inc=1, device_id={"seq": other}, device_id_type=mesh_id)
    pl.semaphore_wait(barrier, 8)

    gather.send_own()

    for block in range(SHARD // 128):
        tile = features[0, 0, :, block * 128 : (block + 1) * 128].astype(F32)
        flipped = jnp.transpose(tile).astype(BF16)
        for piece in range(2):
            place = block * 2 + piece
            transposed[place // 4, place % 4] = flipped[piece * 64 : (piece + 1) * 64]
    own_quarter = pltpu.make_async_copy(
        transposed.at[:, dp], columns.at[tp, :, :, pl.ds(0, 128)], local_sems.at[3]
    )
    own_quarter.start()
    cross = []
    for steps in range(1, DP):
        to = lax.rem(dp + steps, DP)
        copy = remote(
            transposed.at[:, to],
            columns.at[tp, :, :, pl.ds(steps * 128, 128)],
            cross_send.at[steps - 1],
            cross_recv.at[steps - 1],
            dp=to,
        )
        copy.start()
        cross.append(copy)

    in_w.wait()

    def project(owner, half, block=None):
        rows = pl.ds(pl.multiple_of(owner * SHARD + half * HALF, HALF), HALF)
        block = gathered[owner, :, half * HALF : (half + 1) * HALF] if block is None else block
        return jnp.dot(block, w_buf[rows, :], preferred_element_type=F32)

    proj[...] = project(tp, 0, features[0, 0, :, :HALF]) + project(tp, 1, features[0, 0, :, HALF:])
    for half in (0, 1):
        proj[...] += project(*gather.sibling_own(half))

    in_q.wait()
    in_cot.wait()
    gate_tanh = jnp.tanh(jnp.full((8, 128), gate[0], F32))[:1]

    def prepare(head, _):
        lanes = pl.ds(pl.multiple_of(head * HEAD_SIZE, HEAD_SIZE), HEAD_SIZE)
        low = (gate_tanh * cot_buf[:, lanes].astype(F32)).astype(BF16)
        dc_buf[:, lanes] = low
        dc_t[:, lanes] = jnp.transpose(low.astype(F32)).astype(BF16)
        q_t[:, lanes] = jnp.transpose(q_buf[:, lanes].astype(F32)).astype(BF16)
        return 0

    lax.fori_loop(0, HEADS, prepare, 0)

    arrived = [gather.from_left(0), gather.from_right(1)]
    for owner, half in arrived:
        proj[...] += project(owner, half)
    arrived = [gather.from_left(1), gather.from_right(0)]
    for owner, half in arrived:
        proj[...] += project(owner, half)
    for which, half in ((0, 0), (1, 1), (0, 1), (1, 0)):
        proj[...] += project(*gather.sibling_other(which, half))
    arrived = [gather.from_opposite(0), gather.from_opposite(1)]
    for owner, half in arrived:
        proj[...] += project(owner, half)
    for half in (0, 1):
        proj[...] += project(*gather.sibling_other(2, half))

    keys[pl.ds(0, PATCHES), :] = proj[:, :HEAD_SIZE].astype(BF16)
    values[pl.ds(0, PATCHES), :] = proj[:, HEAD_SIZE:].astype(BF16)

    halo = []

    def pass_on(offset):
        for side, rows in enumerate((keys, values)):
            copy = remote(
                rows.at[pl.ds(offset * PATCHES, PATCHES), :],
                rows.at[pl.ds((offset + 1) * PATCHES, PATCHES), :],
                kv_send.at[offset * 2 + side],
                kv_recv.at[offset * 2 + side],
                seq=z_next,
            )
            copy.start()
            halo.append(copy)

    pass_on(0)

    own_quarter.wait()
    for copy in cross:
        copy.wait_recv()
    second = RowGather(
        lambda half: columns.at[tp, pl.ds(half * 2, 2)],
        lambda owner, half: columns.at[owner, pl.ds(half * 2, 2)],
        col_send,
        col_recv,
    )
    second.send_own()

    def score(offset):
        rows = pl.ds(offset * PATCHES, PATCHES)
        nt = (((1,), (1,)), ((), ()))

        def one(head, _):
            lanes = pl.ds(pl.multiple_of(head * HEAD_SIZE, HEAD_SIZE), HEAD_SIZE)
            scores[head, :, rows] = lax.dot_general(
                q_buf[:, lanes], keys[rows, :], nt, preferred_element_type=F32
            )
            d_probs[head, :, rows] = lax.dot_general(
                dc_buf[:, lanes], values[rows, :], nt, preferred_element_type=F32
            )
            return 0

        lax.fori_loop(0, HEADS, one, 0)

    score(0)
    for offset in range(1, REACH):
        for copy in halo[2 * offset - 2 : 2 * offset]:
            copy.wait_recv()
        if offset < REACH - 1:
            pass_on(offset)
        score(offset)

    second.from_left(0)
    second.from_right(1)
    second.from_left(1)
    second.from_right(0)

    lane = lax.broadcasted_iota(jnp.int32, (1, REACH * PATCHES), 1)
    image = z - lax.div(lane, PATCHES)
    is_live = (image >= span_first[0, 0]) & (image <= span_last[0, 0])
    bias = jnp.where(is_live, 0.0, -jnp.inf).astype(F32)

    def attend(head, _):
        lanes = pl.ds(pl.multiple_of(head * HEAD_SIZE, HEAD_SIZE), HEAD_SIZE)
        rows = pl.ds(pl.multiple_of(head * TOKENS, TOKENS), TOKENS)
        logits = scores[head] * SCALE + bias
        exponent = jnp.exp(logits - jnp.max(logits, axis=1, keepdims=True))
        prob = exponent / jnp.sum(exponent, axis=1, keepdims=True)
        prob_low = prob.astype(BF16)
        context = jnp.dot(prob_low, values[...], preferred_element_type=F32)
        att_buf[:, lanes] = (gate_tanh * context).astype(BF16)
        delta = jnp.sum(dc_buf[:, lanes].astype(F32) * context, axis=1, keepdims=True)
        d_score = (prob * (d_probs[head] - delta) * SCALE).astype(BF16)
        dq_buf[:, lanes] = jnp.dot(d_score, keys[...], preferred_element_type=F32).astype(BF16)
        p_buf[rows, :] = prob_low
        ds_buf[rows, :] = d_score
        return 0

    lax.fori_loop(0, HEADS, attend, 0)
    out_att = pltpu.make_async_copy(att_buf, attended_out.at[0], local_sems.at[4])
    out_dq = pltpu.make_async_copy(dq_buf, query_grad_out.at[0], local_sems.at[5])
    out_att.start()
    out_dq.start()

    def partial_gradients(pair):
        window = pl.ds(pair * 2 * PATCHES, 2 * PATCHES)
        for side, (left_ref, right_ref) in enumerate(((q_t, ds_buf), (dc_t, p_buf))):
            both = jnp.dot(left_ref[...], right_ref[:, window], preferred_element_type=F32)
            for index in range(2):
                tile = both[:, index * PATCHES : (index + 1) * PATCHES]
                part[pair * 2 + index, side] = jnp.transpose(tile)

    chain = []

    def hand_back(step):
        for side in range(2):
            copy = remote(
                chain_out.at[step, side],
                chain_in.at[step, side],
                chain_send.at[step * 2 + side],
                chain_recv.at[step * 2 + side],
                seq=z_prev,
            )
            copy.start()
            chain.append(copy)

    partial_gradients(1)
    chain_out[0] = part[REACH - 1].astype(BF16)
    hand_back(0)
    partial_gradients(0)
    second.from_opposite(0)
    second.from_opposite(1)
    for step in range(1, REACH):
        for side in range(2):
            chain[2 * step - 2 + side].wait_recv()
        total = part[REACH - 1 - step] + chain_in[step - 1].astype(F32)
        if step < REACH - 1:
            chain_out[step] = total.astype(BF16)
            hand_back(step)
        else:
            dkv[pl.ds(0, PATCHES), pl.ds(0, HEAD_SIZE)] = total[0].astype(BF16)
            dkv[pl.ds(0, PATCHES), pl.ds(HEAD_SIZE, HEAD_SIZE)] = total[1].astype(BF16)

    shared = []
    for steps in range(1, DP):
        copy = remote(
            dkv.at[pl.ds(0, PATCHES), :],
            dkv.at[pl.ds(steps * PATCHES, PATCHES), :],
            dkv_send.at[steps - 1],
            dkv_recv.at[steps - 1],
            dp=lax.rem(dp + steps, DP),
        )
        copy.start()
        shared.append(copy)
    for half in (0, 1):
        second.sibling_own(half)
        for which in range(3):
            second.sibling_other(which, half)
    for copy in shared:
        copy.wait_recv()

    zs = nz // TP

    def make_term(turn):
        owner = lax.rem(lax.div(z, zs) + turn, TP)
        rows = columns[owner].reshape(zs * 64, DP * PATCHES)
        result = jnp.dot(rows, dkv[...], preferred_element_type=F32)
        term[pl.ds(owner * zs, zs)] = result.reshape(zs, 64, KVC)

    far = nz // 2
    height = 64 // PARTS

    def ring_copy(way, step, piece):
        index = (way * far + step) * PARTS + piece
        rows = pl.ds(piece * height, height)
        return remote(
            ring_out.at[way, step, rows, :],
            ring_in.at[way, step, rows, :],
            ring_send.at[index],
            ring_recv.at[index],
            seq=(z_next, z_prev)[way],
        )

    def target(way, step):
        return lax.rem((z + far - step, z + far + 1 + step)[way], nz)

    make_term(4)
    make_term(5)
    for way in range(2):
        ring_out[way, 0] = term[target(way, 0)].astype(BF16)
        for piece in range(PARTS):
            ring_copy(way, 0, piece).start()
    for turn in (3, 6, 2, 7, 1, 0):
        make_term(turn)

    def ring_step(step, ways):
        for piece in range(PARTS):
            rows = pl.ds(piece * height, height)
            for way in ways:
                ring_copy(way, step - 1, piece).wait_recv()
                total = ring_in[way, step - 1, rows, :].astype(F32) + term[target(way, step), rows, :]
                ring_out[way, step, rows, :] = total.astype(BF16)
                ring_copy(way, step, piece).start()

    def both_ways(step, _):
        ring_step(step, (0, 1))
        return 0

    lax.fori_loop(1, far - 1, both_ways, 0)
    ring_step(far - 1, (0,))

    for piece in range(PARTS):
        ring_copy(0, far - 1, piece).wait_recv()
        ring_copy(1, far - 2, piece).wait_recv()
    total = ring_in[0, far - 1].astype(F32) + ring_in[1, far - 2].astype(F32) + term[z]
    quarter[dp] = total
    last = []
    for steps in range(1, DP):
        copy = remote(
            quarter.at[dp],
            quarter.at[dp],
            last_send.at[steps - 1],
            last_recv.at[steps - 1],
            dp=lax.rem(dp + steps, DP),
        )
        copy.start()
        last.append(copy)

    gather.finish()
    second.finish()
    for copy in cross + halo + chain + shared:
        copy.wait_send()

    def ring_sent(step, _):
        for way in range(2):
            for piece in range(PARTS):
                ring_copy(way, step, piece).wait_send()
        return 0

    lax.fori_loop(0, far - 1, ring_sent, 0)
    for piece in range(PARTS):
        ring_copy(0, far - 1, piece).wait_send()
    out_att.wait()
    out_dq.wait()
    for steps in range(1, DP):
        source = lax.rem(dp + DP - steps, DP)
        remote(
            quarter.at[source],
            quarter.at[source],
            last_send.at[steps - 1],
            last_recv.at[steps - 1],
            dp=source,
        ).wait_recv()
    for copy in last:
        copy.wait_send()
    weight_out[...] = quarter[...].reshape(DP * 64, KVC)


def local(nz, queries, images, kv_weight, gate, cotangent, span_first, span_last):
    far = nz // 2
    zs = nz // TP
    any_space = pl.BlockSpec(memory_space=pl.ANY)
    vmem = pl.BlockSpec(memory_space=pltpu.VMEM)
    smem = pl.BlockSpec(memory_space=pltpu.SMEM)
    dma = pltpu.SemaphoreType.DMA
    rows = REACH * PATCHES
    low = lambda *shape: pltpu.VMEM(shape, BF16)
    wide = lambda *shape: pltpu.VMEM(shape, F32)
    return pl.pallas_call(
        functools.partial(kernel, nz),
        out_shape=(
            jax.ShapeDtypeStruct(queries.shape, BF16),
            jax.ShapeDtypeStruct(queries.shape, BF16),
            jax.ShapeDtypeStruct((DP * 64, KVC), F32),
        ),
        in_specs=[any_space, vmem, any_space, smem, any_space, smem, smem],
        out_specs=(any_space, any_space, vmem),
        scratch_shapes=[
            low(TOKENS, SHARD),
            low(TOKENS, SHARD),
            low(TP * SHARD, KVC),
            low(TP, PATCHES, SHARD),
            wide(PATCHES, KVC),
            low(zs, DP, 64, PATCHES),
            low(TP, zs, 64, DP * PATCHES),
            low(HEAD_SIZE, SHARD),
            low(TOKENS, SHARD),
            low(HEAD_SIZE, SHARD),
            low(rows, HEAD_SIZE),
            low(rows, HEAD_SIZE),
            wide(HEADS, TOKENS, rows),
            wide(HEADS, TOKENS, rows),
            low(HEADS * TOKENS, rows),
            low(HEADS * TOKENS, rows),
            low(TOKENS, SHARD),
            low(TOKENS, SHARD),
            wide(REACH, 2, PATCHES, HEAD_SIZE),
            low(REACH - 1, 2, PATCHES, HEAD_SIZE),
            low(REACH - 1, 2, PATCHES, HEAD_SIZE),
            low(DP * PATCHES, KVC),
            wide(nz, 64, KVC),
            low(2, far, 64, KVC),
            low(2, far, 64, KVC),
            wide(DP, 64, KVC),
            dma((6,)),
            dma((GATHER_COPIES,)),
            dma((GATHER_COPIES,)),
            dma((GATHER_COPIES,)),
            dma((GATHER_COPIES,)),
            dma((DP - 1,)),
            dma((DP - 1,)),
            dma((2 * (REACH - 1),)),
            dma((2 * (REACH - 1),)),
            dma((2 * (REACH - 1),)),
            dma((2 * (REACH - 1),)),
            dma((DP - 1,)),
            dma((DP - 1,)),
            dma((2 * far * PARTS,)),
            dma((2 * far * PARTS,)),
            dma((DP - 1,)),
            dma((DP - 1,)),
        ],
        compiler_params=pltpu.CompilerParams(
            collective_id=0, has_side_effects=True, vmem_limit_bytes=48 * 1024 * 1024
        ),
        name="cross_attention",
    )(queries, images, kv_weight, gate, cotangent, span_first, span_last)


def solution(mesh):
    return jax.shard_map(
        functools.partial(local, mesh.shape["seq"]),
        mesh=mesh,
        in_specs=(
            P("dp", "seq", "tp"),
            P("dp", "seq", None, "tp"),
            P(None, "tp"),
            P(),
            P("dp", "seq", "tp"),
            P("dp", "seq"),
            P("dp", "seq"),
        ),
        out_specs=(P("dp", "seq", "tp"), P("dp", "seq", "tp"), P("seq", "tp")),
        check_vma=False,
    )
```

time: 285 us -> 131 us (0.46)
  waiting for transfers between devices: 209 us -> 0 us
  Pallas kernels: 0 us -> 120 us
  blocking collectives: 20.4 us -> 0 us
  starting transfers between devices: 17.9 us -> 0 us
  between operations: 16.3 us -> 2.59 us
  matrix products: 11.7 us -> 0 us
    reduce_scatter x1 -> x0, waiting for transfers between devices: 147 us -> none  [local(): lax.psum_scatter(local_grad.astype(jnp.bfloat16), 'seq', scatter_dimensio...]
    pallas_call x0 -> x1, Pallas kernels: none -> 120 us  [local(): pl.pallas_call(functools.partial(kernel, nz), out_shape=(jax.ShapeDtypeSt...]
    all_gather x1 -> x0, waiting for transfers between devices: 46.8 us -> none  [local(): all_features = lax.all_gather(features, 'tp', axis=1, tiled=True)]
    psum x1 -> x0, blocking collectives: 20.4 us -> none  [local(): weight_gradient = lax.psum(group_share, 'dp')]
    ppermute x6 -> x0, starting transfers between devices: 17.8 us -> none  [shifted(): lax.ppermute(value, axis, [(source, source + steps) for source in range(f...]
    ppermute x6 -> x0, waiting for transfers between devices: 14.5 us -> none  [shifted(): lax.ppermute(value, axis, [(source, source + steps) for source in range(f...]
    dot_general x8 -> x0, matrix products: 11.7 us -> none  [the longest x1 3.53 us: local(): jnp.dot(all_features, kv_weight, preferred_element_type=jnp.float32)]
    unnamed x22 -> x11, local copies, waits for them, and re-layouts: 3.74 us -> 7.14 us
  transfers between devices with their start and end apart: 8 -> 0, of which waited for: 5 -> 0; matrix products, arithmetic and copies ran while one was open for 2% -> 0% of each run, Pallas kernels for 0% -> 0%
where the time goes in v1:
time: 131 us; the launch traced here: 130 us
  Pallas kernels  120 us (92%)
  local copies, waits for them, and re-layouts  7.14 us (5%)
  between operations  2.59 us (2%)
    pallas_call x1, Pallas kernels, local(): pl.pallas_call(functools.partial(kernel, nz), out_shape=(jax.ShapeDtypeSt...  120 us
    unnamed x11, local copies, waits for them, and re-layouts  7.14 us

profile of v1, /device:TPU:24, one launch (start us, length us, event | category | flops | bytes accessed | tf_op | source)
XLA Modules:
  0.0 129.6 jit_solution(5859297652244282743)
XLA Ops:
  2.6 0.0 copy-start
  2.6 2.2 %copy-done = bf16[8192,256]{1,0:T(8,128)(2,1)S(1)} copy-done((bf16[8192,256]{1,0:T(8,128)(2,1)S(1)}, bf16[8192,256]{1,0:T(8,128)(2,1)}, u32[]{:S(2)}) %copy-start) | copy-done | bytes 4194328
  4.8 0.0 copy-start.1
  4.8 0.9 copy-done.1
  5.7 0.0 copy-start.2
  5.7 0.9 copy-done.2
  6.7 0.0 copy-start.3
  6.7 0.9 copy-done.3
  7.6 119.8 %cross_attention.1 = (bf16[1,128,1024]{2,1,0:T(8,128)(2,1)S(1)}, bf16[1,128,1024]{2,1,0:T(8,128)(2,1)S(1)}, f32[256,256]{1,0:T(8,128)S(1)}) custom-call(bf16[1,128,1024]{2,1,0:T(8,128)(2,1)S(1)} %copy-done.1, bf16[1,1,128,1024]{3,2,1,0:T(8,128)(2,1)S(1)} %copy-done.2, bf16[8192,256]{1,0:T(8,128)(2,1)S(1)} %copy-done, f32[1]{0:T(128)S(6)} %copy.13.gate, ...), custom_call_target="tpu_custom_call" | custom-call | tf_op jit(solution)/shard_map/cross_attention/pallas_call | solution.py:502
  127.5 0.7 copy.16
  128.2 0.7 copy.17
  128.9 0.7 copy.18
Async XLA Ops:
  2.6 2.2 %copy-start = (bf16[8192,256]{1,0:T(8,128)(2,1)S(1)}, bf16[8192,256]{1,0:T(8,128)(2,1)}, u32[]{:S(2)}) copy-start(bf16[8192,256]{1,0:T(8,128)(2,1)} %kv_weight.1) | copy-start | bytes 12582916
  4.8 0.9 copy-start.1
  5.7 0.9 copy-start.2
  6.7 0.9 copy-start.3

commit v2 on v1

--- a/solution.py
+++ b/solution.py
@@ -19,6 +19,8 @@
 KVC = 2 * HEAD_SIZE
 SCALE = HEAD_SIZE ** (-0.5)
 GATHER_COPIES = 14
+GREETINGS = (1, 2, 4, 4)
+STRETCHES = ((9, 7), (8, 7))
 PARTS = 2
 
 BF16 = jnp.bfloat16
@@ -34,6 +36,17 @@
         device_id=where,
         device_id_type=pl.DeviceIdType.MESH,
     )
+
+
+def ring_lanes(nz):
+    lanes, slot = [], 0
+    for way in range(2):
+        base = 0
+        for size in STRETCHES[way]:
+            lanes.append((way, base, size, slot))
+            base, slot = base + size, slot + size
+        assert base == nz // 2 - way
+    return sorted(lanes, key=lambda lane: -lane[1] - lane[2])
 
 
 class RowGather:
@@ -156,14 +169,16 @@
     ring_recv,
     last_send,
     last_recv,
+    greeted,
 ):
     z, tp, dp = lax.axis_index("seq"), lax.axis_index("tp"), lax.axis_index("dp")
     z_next, z_prev = lax.rem(z + 1, nz), lax.rem(z + nz - 1, nz)
 
-    w_copies = []
     in_q = pltpu.make_async_copy(queries.at[0], q_buf, local_sems.at[0])
     in_cot = pltpu.make_async_copy(cotangent.at[0], cot_buf, local_sems.at[1])
     in_w = pltpu.make_async_copy(kv_weight, w_buf, local_sems.at[2])
+    in_f = pltpu.make_async_copy(features.at[0, 0], gathered.at[lax.axis_index('tp')], local_sems.at[6])
+    in_f.start()
     in_q.start()
     in_cot.start()
     in_w.start()
@@ -185,10 +200,22 @@
         pl.semaphore_signal(barrier, inc=1, device_id={"seq": other}, device_id_type=mesh_id)
     pl.semaphore_wait(barrier, 8)
 
+    def greet(turn):
+        for way in range(2):
+            step = GREETINGS[turn]
+            other = lax.rem((z + step, z + nz - step)[way], nz)
+            pl.semaphore_signal(greeted.at[turn * 2 + way], inc=1, device_id={"seq": other}, device_id_type=mesh_id)
+
+    def heard(turn):
+        for way in range(2):
+            pl.semaphore_wait(greeted.at[turn * 2 + way], 1)
+
     gather.send_own()
+    greet(0)
+    in_f.wait()
 
     for block in range(SHARD // 128):
-        tile = features[0, 0, :, block * 128 : (block + 1) * 128].astype(F32)
+        tile = gathered[tp, :, block * 128 : (block + 1) * 128].astype(F32)
         flipped = jnp.transpose(tile).astype(BF16)
         for piece in range(2):
             place = block * 2 + piece
@@ -212,12 +239,12 @@
 
     in_w.wait()
 
-    def project(owner, half, block=None):
+    def project(owner, half):
         rows = pl.ds(pl.multiple_of(owner * SHARD + half * HALF, HALF), HALF)
-        block = gathered[owner, :, half * HALF : (half + 1) * HALF] if block is None else block
+        block = gathered[owner, :, half * HALF : (half + 1) * HALF]
         return jnp.dot(block, w_buf[rows, :], preferred_element_type=F32)
 
-    proj[...] = project(tp, 0, features[0, 0, :, :HALF]) + project(tp, 1, features[0, 0, :, HALF:])
+    proj[...] = project(tp, 0) + project(tp, 1)
     for half in (0, 1):
         proj[...] += project(*gather.sibling_own(half))
 
@@ -234,6 +261,8 @@
         return 0
 
     lax.fori_loop(0, HEADS, prepare, 0)
+    heard(0)
+    greet(1)
 
     arrived = [gather.from_left(0), gather.from_right(1)]
     for owner, half in arrived:
@@ -252,21 +281,23 @@
     keys[pl.ds(0, PATCHES), :] = proj[:, :HEAD_SIZE].astype(BF16)
     values[pl.ds(0, PATCHES), :] = proj[:, HEAD_SIZE:].astype(BF16)
 
+    z_after, z_before = lax.rem(z + 2, nz), lax.rem(z + nz - 2, nz)
     halo = []
 
-    def pass_on(offset):
+    def pass_on(source, offset, to):
         for side, rows in enumerate((keys, values)):
             copy = remote(
+                rows.at[pl.ds(source * PATCHES, PATCHES), :],
                 rows.at[pl.ds(offset * PATCHES, PATCHES), :],
-                rows.at[pl.ds((offset + 1) * PATCHES, PATCHES), :],
-                kv_send.at[offset * 2 + side],
-                kv_recv.at[offset * 2 + side],
-                seq=z_next,
+                kv_send.at[offset * 2 - 2 + side],
+                kv_recv.at[offset * 2 - 2 + side],
+                seq=to,
             )
             copy.start()
             halo.append(copy)
 
-    pass_on(0)
+    pass_on(0, 2, z_after)
+    pass_on(0, 1, z_next)
 
     own_quarter.wait()
     for copy in cross:
@@ -295,13 +326,19 @@
 
         lax.fori_loop(0, HEADS, one, 0)
 
+    heard(1)
+    greet(2)
     score(0)
-    for offset in range(1, REACH):
-        for copy in halo[2 * offset - 2 : 2 * offset]:
-            copy.wait_recv()
-        if offset < REACH - 1:
-            pass_on(offset)
-        score(offset)
+    for copy in halo[:2]:
+        copy.wait_recv()
+    pass_on(2, 3, z_next)
+    score(2)
+    for copy in halo[2:4]:
+        copy.wait_recv()
+    score(1)
+    for copy in halo[4:]:
+        copy.wait_recv()
+    score(3)
 
     second.from_left(0)
     second.from_right(1)
@@ -318,7 +355,7 @@
         rows = pl.ds(pl.multiple_of(head * TOKENS, TOKENS), TOKENS)
         logits = scores[head] * SCALE + bias
         exponent = jnp.exp(logits - jnp.max(logits, axis=1, keepdims=True))
-        prob = exponent / jnp.sum(exponent, axis=1, keepdims=True)
+        prob = exponent * (1.0 / jnp.sum(exponent, axis=1, keepdims=True))
         prob_low = prob.astype(BF16)
         context = jnp.dot(prob_low, values[...], preferred_element_type=F32)
         att_buf[:, lanes] = (gate_tanh * context).astype(BF16)
@@ -329,6 +366,8 @@
         ds_buf[rows, :] = d_score
         return 0
 
+    heard(2)
+    greet(3)
     lax.fori_loop(0, HEADS, attend, 0)
     out_att = pltpu.make_async_copy(att_buf, attended_out.at[0], local_sems.at[4])
     out_dq = pltpu.make_async_copy(dq_buf, query_grad_out.at[0], local_sems.at[5])
@@ -345,34 +384,35 @@
 
     chain = []
 
-    def hand_back(step):
+    def hand_back(step, to):
         for side in range(2):
             copy = remote(
                 chain_out.at[step, side],
                 chain_in.at[step, side],
                 chain_send.at[step * 2 + side],
                 chain_recv.at[step * 2 + side],
-                seq=z_prev,
+                seq=to,
             )
             copy.start()
             chain.append(copy)
 
     partial_gradients(1)
-    chain_out[0] = part[REACH - 1].astype(BF16)
-    hand_back(0)
+    chain_out[0] = part[3].astype(BF16)
+    hand_back(0, z_prev)
     partial_gradients(0)
+    chain_out[2] = part[1].astype(BF16)
+    hand_back(2, z_prev)
     second.from_opposite(0)
     second.from_opposite(1)
-    for step in range(1, REACH):
-        for side in range(2):
-            chain[2 * step - 2 + side].wait_recv()
-        total = part[REACH - 1 - step] + chain_in[step - 1].astype(F32)
-        if step < REACH - 1:
-            chain_out[step] = total.astype(BF16)
-            hand_back(step)
-        else:
-            dkv[pl.ds(0, PATCHES), pl.ds(0, HEAD_SIZE)] = total[0].astype(BF16)
-            dkv[pl.ds(0, PATCHES), pl.ds(HEAD_SIZE, HEAD_SIZE)] = total[1].astype(BF16)
+    for copy in chain[:2]:
+        copy.wait_recv()
+    chain_out[1] = (part[2] + chain_in[0].astype(F32)).astype(BF16)
+    hand_back(1, z_before)
+    for copy in chain[2:]:
+        copy.wait_recv()
+    total = part[0] + chain_in[2].astype(F32) + chain_in[1].astype(F32)
+    dkv[pl.ds(0, PATCHES), pl.ds(0, HEAD_SIZE)] = total[0].astype(BF16)
+    dkv[pl.ds(0, PATCHES), pl.ds(HEAD_SIZE, HEAD_SIZE)] = total[1].astype(BF16)
 
     shared = []
     for steps in range(1, DP):
@@ -392,6 +432,8 @@
     for copy in shared:
         copy.wait_recv()
 
+    heard(3)
+
     zs = nz // TP
 
     def make_term(turn):
@@ -400,52 +442,60 @@
         result = jnp.dot(rows, dkv[...], preferred_element_type=F32)
         term[pl.ds(owner * zs, zs)] = result.reshape(zs, 64, KVC)
 
-    far = nz // 2
+    lanes = ring_lanes(nz)
     height = 64 // PARTS
 
-    def ring_copy(way, step, piece):
-        index = (way * far + step) * PARTS + piece
+    def target(lane, step):
+        way, base, size, _ = lane
+        away = base + size - step
+        return lax.rem((z + away, z + nz - away)[way], nz)
+
+    def ring_copy(lane, step, piece):
+        way, _, size, first = lane
         rows = pl.ds(piece * height, height)
+        to = target(lane, step) if step == size - 1 else (z_next, z_prev)[way]
+        place = first + step
         return remote(
-            ring_out.at[way, step, rows, :],
-            ring_in.at[way, step, rows, :],
-            ring_send.at[index],
-            ring_recv.at[index],
-            seq=(z_next, z_prev)[way],
+            ring_out.at[place, rows, :],
+            ring_in.at[place, rows, :],
+            ring_send.at[place * PARTS + piece],
+            ring_recv.at[place * PARTS + piece],
+            seq=to,
         )
 
-    def target(way, step):
-        return lax.rem((z + far - step, z + far + 1 + step)[way], nz)
-
-    make_term(4)
-    make_term(5)
-    for way in range(2):
-        ring_out[way, 0] = term[target(way, 0)].astype(BF16)
-        for piece in range(PARTS):
-            ring_copy(way, 0, piece).start()
-    for turn in (3, 6, 2, 7, 1, 0):
-        make_term(turn)
-
-    def ring_step(step, ways):
+    def ring_step(lane, step):
+        place = lane[3] + step
         for piece in range(PARTS):
             rows = pl.ds(piece * height, height)
-            for way in ways:
-                ring_copy(way, step - 1, piece).wait_recv()
-                total = ring_in[way, step - 1, rows, :].astype(F32) + term[target(way, step), rows, :]
-                ring_out[way, step, rows, :] = total.astype(BF16)
-                ring_copy(way, step, piece).start()
-
-    def both_ways(step, _):
-        ring_step(step, (0, 1))
-        return 0
-
-    lax.fori_loop(1, far - 1, both_ways, 0)
-    ring_step(far - 1, (0,))
-
-    for piece in range(PARTS):
-        ring_copy(0, far - 1, piece).wait_recv()
-        ring_copy(1, far - 2, piece).wait_recv()
-    total = ring_in[0, far - 1].astype(F32) + ring_in[1, far - 2].astype(F32) + term[z]
+            total = term[target(lane, step), rows, :]
+            if step:
+                ring_copy(lane, step - 1, piece).wait_recv()
+                total += ring_in[place - 1, rows, :].astype(F32)
+            ring_out[place, rows, :] = total.astype(BF16)
+            ring_copy(lane, step, piece).start()
+
+    for turn in (4, 5):
+        make_term(turn)
+    for lane in lanes[:2]:
+        ring_step(lane, 0)
+    for turn in (3, 2, 6):
+        make_term(turn)
+    for lane in lanes[2:4]:
+        ring_step(lane, 0)
+    for turn in (1, 7, 0):
+        make_term(turn)
+    for lane in lanes[4:]:
+        ring_step(lane, 0)
+    for step in range(1, max(lane[2] for lane in lanes)):
+        for lane in lanes:
+            if step < lane[2]:
+                ring_step(lane, step)
+
+    total = term[z]
+    for lane in lanes[::-1]:
+        for piece in range(PARTS):
+            ring_copy(lane, lane[2] - 1, piece).wait_recv()
+        total += ring_in[lane[3] + lane[2] - 1].astype(F32)
     quarter[dp] = total
     last = []
     for steps in range(1, DP):
@@ -464,15 +514,10 @@
     for copy in cross + halo + chain + shared:
         copy.wait_send()
 
-    def ring_sent(step, _):
-        for way in range(2):
+    for lane in lanes:
+        for step in range(lane[2]):
             for piece in range(PARTS):
-                ring_copy(way, step, piece).wait_send()
-        return 0
-
-    lax.fori_loop(0, far - 1, ring_sent, 0)
-    for piece in range(PARTS):
-        ring_copy(0, far - 1, piece).wait_send()
+                ring_copy(lane, step, piece).wait_send()
     out_att.wait()
     out_dq.wait()
     for steps in range(1, DP):
@@ -490,9 +535,8 @@
 
 
 def local(nz, queries, images, kv_weight, gate, cotangent, span_first, span_last):
-    far = nz // 2
     zs = nz // TP
-    any_space = pl.BlockSpec(memory_space=pl.ANY)
+    any_space = pl.BlockSpec(memory_space=pltpu.HBM)
     vmem = pl.BlockSpec(memory_space=pltpu.VMEM)
     smem = pl.BlockSpec(memory_space=pltpu.SMEM)
     dma = pltpu.SemaphoreType.DMA
@@ -506,7 +550,7 @@
             jax.ShapeDtypeStruct(queries.shape, BF16),
             jax.ShapeDtypeStruct((DP * 64, KVC), F32),
         ),
-        in_specs=[any_space, vmem, any_space, smem, any_space, smem, smem],
+        in_specs=[any_space, any_space, any_space, smem, any_space, smem, smem],
         out_specs=(any_space, any_space, vmem),
         scratch_shapes=[
             low(TOKENS, SHARD),
@@ -532,10 +576,10 @@
             low(REACH - 1, 2, PATCHES, HEAD_SIZE),
             low(DP * PATCHES, KVC),
             wide(nz, 64, KVC),
-            low(2, far, 64, KVC),
-            low(2, far, 64, KVC),
+            low(nz - 1, 64, KVC),
+            low(nz - 1, 64, KVC),
             wide(DP, 64, KVC),
-            dma((6,)),
+            dma((7,)),
             dma((GATHER_COPIES,)),
             dma((GATHER_COPIES,)),
             dma((GATHER_COPIES,)),
@@ -548,13 +592,14 @@
             dma((2 * (REACH - 1),)),
             dma((DP - 1,)),
             dma((DP - 1,)),
-            dma((2 * far * PARTS,)),
-            dma((2 * far * PARTS,)),
+            dma(((nz - 1) * PARTS,)),
+            dma(((nz - 1) * PARTS,)),
             dma((DP - 1,)),
             dma((DP - 1,)),
+            pltpu.SemaphoreType.REGULAR((2 * len(GREETINGS),)),
         ],
         compiler_params=pltpu.CompilerParams(
-            collective_id=0, has_side_effects=True, vmem_limit_bytes=48 * 1024 * 1024
+            collective_id=0, has_side_effects=True, vmem_limit_bytes=67043328
         ),
         name="cross_attention",
     )(queries, images, kv_weight, gate, cotangent, span_first, span_last)

time: 131 us -> 108 us (0.82)
  the two profiles are of different devices: /device:TPU:24 before, /device:TPU:32 now
where the time goes in v2:
time: 108 us
  Pallas kernels  100 us (93%)
  local copies, waits for them, and re-layouts  5.01 us (5%)
  between operations  2.58 us (2%)
    pallas_call x1, Pallas kernels, local(): pl.pallas_call(functools.partial(kernel, nz), out_shape=(jax.ShapeDtypeSt...  100 us
    unnamed x3, local copies, waits for them, and re-layouts  5.01 us

profile of v2, /device:TPU:32, one launch (start us, length us, event | category | flops | bytes accessed | tf_op | source)
XLA Modules:
  0.0 107.9 jit_solution(2799374806106255085)
XLA Ops:
  2.6 100.3 %cross_attention.1 = (bf16[1,128,1024]{2,1,0:T(8,128)(2,1)}, bf16[1,128,1024]{2,1,0:T(8,128)(2,1)}, f32[256,256]{1,0:T(8,128)}) custom-call(bf16[1,128,1024]{2,1,0:T(8,128)(2,1)} %queries.1, bf16[1,1,128,1024]{3,2,1,0:T(8,128)(2,1)} %features.1, bf16[8192,256]{1,0:T(8,128)(2,1)} %kv_weight.1, f32[1]{0:T(128)S(6)} %copy.13.gate, ...), custom_call_target="tpu_custom_call" | custom-call | tf_op jit(solution)/shard_map/cross_attention/pallas_call | solution.py:546
  102.9 1.7 %copy.16 = bf16[1,128,1024]{2,1,0:T(8,128)(2,1)} copy(bf16[1,128,1024]{2,1,0:T(8,128)(2,1)} %get-tuple-element.6) | data formatting | bytes 524288
  104.6 1.7 %copy.17 = bf16[1,128,1024]{2,1,0:T(8,128)(2,1)} copy(bf16[1,128,1024]{2,1,0:T(8,128)(2,1)} %get-tuple-element.7) | data formatting | bytes 524288
  106.3 1.7 %copy.18 = f32[256,256]{1,0:T(8,128)} copy(f32[256,256]{1,0:T(8,128)} %get-tuple-element.8) | data formatting | bytes 524288

commit v3 on v2

--- a/solution.py
+++ b/solution.py
@@ -260,7 +260,7 @@
         q_t[:, lanes] = jnp.transpose(q_buf[:, lanes].astype(F32)).astype(BF16)
         return 0
 
-    lax.fori_loop(0, HEADS, prepare, 0)
+    lax.fori_loop(0, HEADS, prepare, 0, unroll=True)
     heard(0)
     greet(1)
 
@@ -324,7 +324,7 @@
             )
             return 0
 
-        lax.fori_loop(0, HEADS, one, 0)
+        lax.fori_loop(0, HEADS, one, 0, unroll=True)
 
     heard(1)
     greet(2)
@@ -368,7 +368,7 @@
 
     heard(2)
     greet(3)
-    lax.fori_loop(0, HEADS, attend, 0)
+    lax.fori_loop(0, HEADS, attend, 0, unroll=True)
     out_att = pltpu.make_async_copy(att_buf, attended_out.at[0], local_sems.at[4])
     out_dq = pltpu.make_async_copy(dq_buf, query_grad_out.at[0], local_sems.at[5])
     out_att.start()
@@ -496,7 +496,7 @@
         for piece in range(PARTS):
             ring_copy(lane, lane[2] - 1, piece).wait_recv()
         total += ring_in[lane[3] + lane[2] - 1].astype(F32)
-    quarter[dp] = total
+    quarter[dp] = total.astype(BF16)
     last = []
     for steps in range(1, DP):
         copy = remote(
@@ -531,7 +531,7 @@
         ).wait_recv()
     for copy in last:
         copy.wait_send()
-    weight_out[...] = quarter[...].reshape(DP * 64, KVC)
+    weight_out[...] = quarter[...].reshape(DP * 64, KVC).astype(F32)
 
 
 def local(nz, queries, images, kv_weight, gate, cotangent, span_first, span_last):
@@ -578,7 +578,7 @@
             wide(nz, 64, KVC),
             low(nz - 1, 64, KVC),
             low(nz - 1, 64, KVC),
-            wide(DP, 64, KVC),
+            low(DP, 64, KVC),
             dma((7,)),
             dma((GATHER_COPIES,)),
             dma((GATHER_COPIES,)),

time: 108 us -> 103 us (0.954)
  the two profiles are of different devices: /device:TPU:32 before, /device:TPU:24 now
where the time goes in v3:
time: 103 us
  Pallas kernels  95.3 us (93%)
  local copies, waits for them, and re-layouts  5.01 us (5%)
  between operations  2.58 us (3%)
    pallas_call x1, Pallas kernels, local(): pl.pallas_call(functools.partial(kernel, nz), out_shape=(jax.ShapeDtypeSt...  95.3 us
    unnamed x3, local copies, waits for them, and re-layouts  5.01 us

profile of v3, /device:TPU:24, one launch (start us, length us, event | category | flops | bytes accessed | tf_op | source)
XLA Modules:
  0.0 102.9 jit_solution(15279109009036179443)
XLA Ops:
  2.6 95.3 %cross_attention.1 = (bf16[1,128,1024]{2,1,0:T(8,128)(2,1)}, bf16[1,128,1024]{2,1,0:T(8,128)(2,1)}, f32[256,256]{1,0:T(8,128)}) custom-call(bf16[1,128,1024]{2,1,0:T(8,128)(2,1)} %queries.1, bf16[1,1,128,1024]{3,2,1,0:T(8,128)(2,1)} %features.1, bf16[8192,256]{1,0:T(8,128)(2,1)} %kv_weight.1, f32[1]{0:T(128)S(6)} %copy.13.gate, ...), custom_call_target="tpu_custom_call" | custom-call | tf_op jit(solution)/shard_map/cross_attention/pallas_call | solution.py:546
  97.9 1.7 %copy.16 = bf16[1,128,1024]{2,1,0:T(8,128)(2,1)} copy(bf16[1,128,1024]{2,1,0:T(8,128)(2,1)} %get-tuple-element.6) | data formatting | bytes 524288
  99.6 1.7 %copy.17 = bf16[1,128,1024]{2,1,0:T(8,128)(2,1)} copy(bf16[1,128,1024]{2,1,0:T(8,128)(2,1)} %get-tuple-element.7) | data formatting | bytes 524288
  101.2 1.7 %copy.18 = f32[256,256]{1,0:T(8,128)} copy(f32[256,256]{1,0:T(8,128)} %get-tuple-element.8) | data formatting | bytes 524288

commit v4 on v3

--- a/solution.py
+++ b/solution.py
@@ -415,7 +415,7 @@
     dkv[pl.ds(0, PATCHES), pl.ds(HEAD_SIZE, HEAD_SIZE)] = total[1].astype(BF16)
 
     shared = []
-    for steps in range(1, DP):
+    for steps in (2, 1, 3):
         copy = remote(
             dkv.at[pl.ds(0, PATCHES), :],
             dkv.at[pl.ds(steps * PATCHES, PATCHES), :],
@@ -498,7 +498,7 @@
         total += ring_in[lane[3] + lane[2] - 1].astype(F32)
     quarter[dp] = total.astype(BF16)
     last = []
-    for steps in range(1, DP):
+    for steps in (2, 1, 3):
         copy = remote(
             quarter.at[dp],
             quarter.at[dp],
@@ -542,6 +542,7 @@
     dma = pltpu.SemaphoreType.DMA
     rows = REACH * PATCHES
     low = lambda *shape: pltpu.VMEM(shape, BF16)
+    hbm = lambda array: pltpu.with_memory_space_constraint(array, pltpu.HBM)
     wide = lambda *shape: pltpu.VMEM(shape, F32)
     return pl.pallas_call(
         functools.partial(kernel, nz),
@@ -599,10 +600,10 @@
             pltpu.SemaphoreType.REGULAR((2 * len(GREETINGS),)),
         ],
         compiler_params=pltpu.CompilerParams(
-            collective_id=0, has_side_effects=True, vmem_limit_bytes=67043328
+            collective_id=0, has_side_effects=True, vmem_limit_bytes=48 * 1024 * 1024
         ),
         name="cross_attention",
-    )(queries, images, kv_weight, gate, cotangent, span_first, span_last)
+    )(hbm(queries), hbm(images), hbm(kv_weight), gate, hbm(cotangent), span_first, span_last)
 
 
 def solution(mesh):

time: 103 us -> 101 us (0.981); the launches traced: 103 us -> 98.9 us
  local copies, waits for them, and re-layouts: 5.01 us -> 2.11 us
  Pallas kernels: 95.3 us -> 94.2 us
    unnamed x3, local copies, waits for them, and re-layouts: 5.01 us -> 2.11 us
    pallas_call x1, Pallas kernels: 95.3 us -> 94.2 us  [local(): pl.pallas_call(functools.partial(kernel, nz), out_shape=(jax.ShapeDtypeSt...]
where the time goes in v4:
time: 101 us; the launch traced here: 98.9 us
  Pallas kernels  94.2 us (93%)
  between operations  2.58 us (3%)
  local copies, waits for them, and re-layouts  2.11 us (2%)
    pallas_call x1, Pallas kernels, local(): pl.pallas_call(functools.partial(kernel, nz), out_shape=(jax.ShapeDtypeSt...  94.2 us
    unnamed x3, local copies, waits for them, and re-layouts  2.11 us

profile of v4, /device:TPU:24, one launch (start us, length us, event | category | flops | bytes accessed | tf_op | source)
XLA Modules:
  0.0 98.9 jit_solution(6865498576232064758)
XLA Ops:
  2.6 94.2 %cross_attention.1 = (bf16[1,128,1024]{2,1,0:T(8,128)(2,1)S(1)}, bf16[1,128,1024]{2,1,0:T(8,128)(2,1)S(1)}, f32[256,256]{1,0:T(8,128)S(1)}) custom-call(bf16[1,128,1024]{2,1,0:T(8,128)(2,1)} %queries.1, bf16[1,1,128,1024]{3,2,1,0:T(8,128)(2,1)} %features.1, bf16[8192,256]{1,0:T(8,128)(2,1)} %kv_weight.1, f32[1]{0:T(128)S(6)} %copy.13.gate, ...), custom_call_target="tpu_custom_call" | custom-call | tf_op jit(solution)/shard_map/cross_attention/pallas_call | solution.py:547
  96.8 0.7 copy.16
  97.5 0.7 copy.17
  98.2 0.7 copy.18

commit v5 on v4

--- a/solution.py
+++ b/solution.py
@@ -20,7 +20,8 @@
 SCALE = HEAD_SIZE ** (-0.5)
 GATHER_COPIES = 14
 GREETINGS = (1, 2, 4, 4)
-STRETCHES = ((9, 7), (8, 7))
+PAIR = 2
+STRETCHES = ((5, 3), (4, 3))
 PARTS = 2
 
 BF16 = jnp.bfloat16
@@ -45,7 +46,7 @@
         for size in STRETCHES[way]:
             lanes.append((way, base, size, slot))
             base, slot = base + size, slot + size
-        assert base == nz // 2 - way
+        assert base == nz // (2 * PAIR) - way
     return sorted(lanes, key=lambda lane: -lane[1] - lane[2])
 
 
@@ -173,6 +174,13 @@
 ):
     z, tp, dp = lax.axis_index("seq"), lax.axis_index("tp"), lax.axis_index("dp")
     z_next, z_prev = lax.rem(z + 1, nz), lax.rem(z + nz - 1, nz)
+    z_after, z_before = lax.rem(z + 2, nz), lax.rem(z + nz - 2, nz)
+    parity = lax.rem(z, PAIR)
+    partner = z + 1 - 2 * parity
+    peers = [(side, steps) for side, steps in ((1, 2), (0, 2), (1, 1), (1, 3), (0, 1), (0, 3), (1, 0))]
+
+    def peer(side, steps):
+        return {"seq": (z, partner)[side], "dp": lax.rem(dp + steps, DP)}
 
     in_q = pltpu.make_async_copy(queries.at[0], q_buf, local_sems.at[0])
     in_cot = pltpu.make_async_copy(cotangent.at[0], cot_buf, local_sems.at[1])
@@ -196,9 +204,10 @@
     for steps in range(1, DP):
         other = lax.rem(dp + steps, DP)
         pl.semaphore_signal(barrier, inc=1, device_id={"dp": other}, device_id_type=mesh_id)
+        pl.semaphore_signal(barrier, inc=1, device_id=peer(1, steps), device_id_type=mesh_id)
     for other in (z_next, z_prev):
         pl.semaphore_signal(barrier, inc=1, device_id={"seq": other}, device_id_type=mesh_id)
-    pl.semaphore_wait(barrier, 8)
+    pl.semaphore_wait(barrier, 11)
 
     def greet(turn):
         for way in range(2):
@@ -219,20 +228,22 @@
         flipped = jnp.transpose(tile).astype(BF16)
         for piece in range(2):
             place = block * 2 + piece
-            transposed[place // 4, place % 4] = flipped[piece * 64 : (piece + 1) * 64]
+            row = place // DP
+            transposed[row % PAIR, row // PAIR, place % DP] = flipped[piece * 64 : (piece + 1) * 64]
     own_quarter = pltpu.make_async_copy(
-        transposed.at[:, dp], columns.at[tp, :, :, pl.ds(0, 128)], local_sems.at[3]
+        transposed.at[parity, :, dp], columns.at[tp, :, :, pl.ds(0, 128)], local_sems.at[3]
     )
     own_quarter.start()
     cross = []
-    for steps in range(1, DP):
-        to = lax.rem(dp + steps, DP)
+    for side, steps in peers:
+        place = side * DP + steps
+        where = peer(side, steps)
         copy = remote(
-            transposed.at[:, to],
-            columns.at[tp, :, :, pl.ds(steps * 128, 128)],
-            cross_send.at[steps - 1],
-            cross_recv.at[steps - 1],
-            dp=to,
+            transposed.at[(parity, 1 - parity)[side], :, where["dp"]],
+            columns.at[tp, :, :, pl.ds(place * 128, 128)],
+            cross_send.at[place - 1],
+            cross_recv.at[place - 1],
+            **where,
         )
         copy.start()
         cross.append(copy)
@@ -281,7 +292,6 @@
     keys[pl.ds(0, PATCHES), :] = proj[:, :HEAD_SIZE].astype(BF16)
     values[pl.ds(0, PATCHES), :] = proj[:, HEAD_SIZE:].astype(BF16)
 
-    z_after, z_before = lax.rem(z + 2, nz), lax.rem(z + nz - 2, nz)
     halo = []
 
     def pass_on(source, offset, to):
@@ -303,8 +313,8 @@
     for copy in cross:
         copy.wait_recv()
     second = RowGather(
-        lambda half: columns.at[tp, pl.ds(half * 2, 2)],
-        lambda owner, half: columns.at[owner, pl.ds(half * 2, 2)],
+        lambda half: columns.at[tp, pl.ds(half, 1)],
+        lambda owner, half: columns.at[owner, pl.ds(half, 1)],
         col_send,
         col_recv,
     )
@@ -415,13 +425,14 @@
     dkv[pl.ds(0, PATCHES), pl.ds(HEAD_SIZE, HEAD_SIZE)] = total[1].astype(BF16)
 
     shared = []
-    for steps in (2, 1, 3):
+    for side, steps in peers:
+        place = side * DP + steps
         copy = remote(
             dkv.at[pl.ds(0, PATCHES), :],
-            dkv.at[pl.ds(steps * PATCHES, PATCHES), :],
-            dkv_send.at[steps - 1],
-            dkv_recv.at[steps - 1],
-            dp=lax.rem(dp + steps, DP),
+            dkv.at[pl.ds(place * PATCHES, PATCHES), :],
+            dkv_send.at[place - 1],
+            dkv_recv.at[place - 1],
+            **peer(side, steps),
         )
         copy.start()
         shared.append(copy)
@@ -434,11 +445,13 @@
 
     heard(3)
 
-    zs = nz // TP
+    zs = nz // TP // PAIR
+    members = nz // PAIR
+    member = lax.div(z, PAIR)
 
     def make_term(turn):
-        owner = lax.rem(lax.div(z, zs) + turn, TP)
-        rows = columns[owner].reshape(zs * 64, DP * PATCHES)
+        owner = lax.rem(lax.div(member, zs) + turn, TP)
+        rows = columns[owner].reshape(zs * 64, PAIR * DP * PATCHES)
         result = jnp.dot(rows, dkv[...], preferred_element_type=F32)
         term[pl.ds(owner * zs, zs)] = result.reshape(zs, 64, KVC)
 
@@ -448,12 +461,12 @@
     def target(lane, step):
         way, base, size, _ = lane
         away = base + size - step
-        return lax.rem((z + away, z + nz - away)[way], nz)
+        return lax.rem((member + away, member + members - away)[way], members)
 
     def ring_copy(lane, step, piece):
         way, _, size, first = lane
         rows = pl.ds(piece * height, height)
-        to = target(lane, step) if step == size - 1 else (z_next, z_prev)[way]
+        to = target(lane, step) * PAIR + parity if step == size - 1 else (z_after, z_before)[way]
         place = first + step
         return remote(
             ring_out.at[place, rows, :],
@@ -491,7 +504,7 @@
             if step < lane[2]:
                 ring_step(lane, step)
 
-    total = term[z]
+    total = term[member]
     for lane in lanes[::-1]:
         for piece in range(PARTS):
             ring_copy(lane, lane[2] - 1, piece).wait_recv()
@@ -559,8 +572,8 @@
             low(TP * SHARD, KVC),
             low(TP, PATCHES, SHARD),
             wide(PATCHES, KVC),
-            low(zs, DP, 64, PATCHES),
-            low(TP, zs, 64, DP * PATCHES),
+            low(PAIR, zs // PAIR, DP, 64, PATCHES),
+            low(TP, zs // PAIR, 64, PAIR * DP * PATCHES),
             low(HEAD_SIZE, SHARD),
             low(TOKENS, SHARD),
             low(HEAD_SIZE, SHARD),
@@ -575,26 +588,26 @@
             wide(REACH, 2, PATCHES, HEAD_SIZE),
             low(REACH - 1, 2, PATCHES, HEAD_SIZE),
             low(REACH - 1, 2, PATCHES, HEAD_SIZE),
-            low(DP * PATCHES, KVC),
-            wide(nz, 64, KVC),
-            low(nz - 1, 64, KVC),
-            low(nz - 1, 64, KVC),
+            low(PAIR * DP * PATCHES, KVC),
+            wide(nz // PAIR, 64, KVC),
+            low(nz // PAIR - 1, 64, KVC),
+            low(nz // PAIR - 1, 64, KVC),
             low(DP, 64, KVC),
             dma((7,)),
             dma((GATHER_COPIES,)),
             dma((GATHER_COPIES,)),
             dma((GATHER_COPIES,)),
             dma((GATHER_COPIES,)),
-            dma((DP - 1,)),
-            dma((DP - 1,)),
+            dma((PAIR * DP - 1,)),
+            dma((PAIR * DP - 1,)),
             dma((2 * (REACH - 1),)),
             dma((2 * (REACH - 1),)),
             dma((2 * (REACH - 1),)),
             dma((2 * (REACH - 1),)),
-            dma((DP - 1,)),
-            dma((DP - 1,)),
-            dma(((nz - 1) * PARTS,)),
-            dma(((nz - 1) * PARTS,)),
+            dma((PAIR * DP - 1,)),
+            dma((PAIR * DP - 1,)),
+            dma(((nz // PAIR - 1) * PARTS,)),
+            dma(((nz // PAIR - 1) * PARTS,)),
             dma((DP - 1,)),
             dma((DP - 1,)),
             pltpu.SemaphoreType.REGULAR((2 * len(GREETINGS),)),

time: 101 us -> 98.2 us (0.972); the launches traced: 98.9 us -> 97.2 us
  Pallas kernels: 94.2 us -> 92.5 us
    pallas_call x1, Pallas kernels: 94.2 us -> 92.5 us  [local(): pl.pallas_call(functools.partial(kernel, nz), out_shape=(jax.ShapeDtypeSt...]
where the time goes in v5:
time: 98.2 us; the launch traced here: 97.2 us
  Pallas kernels  92.5 us (94%)
  between operations  2.58 us (3%)
  local copies, waits for them, and re-layouts  2.11 us (2%)
    pallas_call x1, Pallas kernels, local(): pl.pallas_call(functools.partial(kernel, nz), out_shape=(jax.ShapeDtypeSt...  92.5 us
    unnamed x3, local copies, waits for them, and re-layouts  2.11 us

profile of v5, /device:TPU:24, one launch (start us, length us, event | category | flops | bytes accessed | tf_op | source)
XLA Modules:
  0.0 97.2 jit_solution(12274548307426500807)
XLA Ops:
  2.6 92.5 %cross_attention.1 = (bf16[1,128,1024]{2,1,0:T(8,128)(2,1)S(1)}, bf16[1,128,1024]{2,1,0:T(8,128)(2,1)S(1)}, f32[256,256]{1,0:T(8,128)S(1)}) custom-call(bf16[1,128,1024]{2,1,0:T(8,128)(2,1)} %queries.1, bf16[1,1,128,1024]{3,2,1,0:T(8,128)(2,1)} %features.1, bf16[8192,256]{1,0:T(8,128)(2,1)} %kv_weight.1, f32[1]{0:T(128)S(6)} %copy.13.gate, ...), custom_call_target="tpu_custom_call" | custom-call | tf_op jit(solution)/shard_map/cross_attention/pallas_call | solution.py:560
  95.1 0.7 copy.16
  95.8 0.7 copy.17
  96.5 0.7 copy.18

commit v6 on v5

--- a/solution.py
+++ b/solution.py
@@ -294,8 +294,9 @@
 
     halo = []
 
-    def pass_on(source, offset, to):
-        for side, rows in enumerate((keys, values)):
+    def pass_on(source, offset, to, sides=(0, 1)):
+        for side in sides:
+            rows = (keys, values)[side]
             copy = remote(
                 rows.at[pl.ds(source * PATCHES, PATCHES), :],
                 rows.at[pl.ds(offset * PATCHES, PATCHES), :],
@@ -339,9 +340,9 @@
     heard(1)
     greet(2)
     score(0)
-    for copy in halo[:2]:
-        copy.wait_recv()
-    pass_on(2, 3, z_next)
+    for side in range(2):
+        halo[side].wait_recv()
+        pass_on(2, 3, z_next, (side,))
     score(2)
     for copy in halo[2:4]:
         copy.wait_recv()
@@ -384,9 +385,10 @@
     out_att.start()
     out_dq.start()
 
-    def partial_gradients(pair):
+    def partial_gradients(pair, sides=(0, 1)):
         window = pl.ds(pair * 2 * PATCHES, 2 * PATCHES)
-        for side, (left_ref, right_ref) in enumerate(((q_t, ds_buf), (dc_t, p_buf))):
+        for side in sides:
+            left_ref, right_ref = ((q_t, ds_buf), (dc_t, p_buf))[side]
             both = jnp.dot(left_ref[...], right_ref[:, window], preferred_element_type=F32)
             for index in range(2):
                 tile = both[:, index * PATCHES : (index + 1) * PATCHES]
@@ -394,8 +396,8 @@
 
     chain = []
 
-    def hand_back(step, to):
-        for side in range(2):
+    def hand_back(step, to, sides=(0, 1)):
+        for side in sides:
             copy = remote(
                 chain_out.at[step, side],
                 chain_in.at[step, side],
@@ -406,18 +408,19 @@
             copy.start()
             chain.append(copy)
 
-    partial_gradients(1)
-    chain_out[0] = part[3].astype(BF16)
-    hand_back(0, z_prev)
+    for side in range(2):
+        partial_gradients(1, (side,))
+        chain_out[0, side] = part[3, side].astype(BF16)
+        hand_back(0, z_prev, (side,))
     partial_gradients(0)
     chain_out[2] = part[1].astype(BF16)
     hand_back(2, z_prev)
     second.from_opposite(0)
     second.from_opposite(1)
-    for copy in chain[:2]:
-        copy.wait_recv()
-    chain_out[1] = (part[2] + chain_in[0].astype(F32)).astype(BF16)
-    hand_back(1, z_before)
+    for side in range(2):
+        chain[side].wait_recv()
+        chain_out[1, side] = (part[2, side] + chain_in[0, side].astype(F32)).astype(BF16)
+        hand_back(1, z_before, (side,))
     for copy in chain[2:]:
         copy.wait_recv()
     total = part[0] + chain_in[2].astype(F32) + chain_in[1].astype(F32)

time: 98.2 us -> 96.9 us (0.987)
  Pallas kernels: 92.5 us -> 90.6 us
    pallas_call x1, Pallas kernels: 92.5 us -> 90.6 us  [local(): pl.pallas_call(functools.partial(kernel, nz), out_shape=(jax.ShapeDtypeSt...]
where the time goes in v6:
time: 96.9 us; the launch traced here: 95.3 us
  Pallas kernels  90.6 us (93%)
  between operations  2.58 us (3%)
  local copies, waits for them, and re-layouts  2.11 us (2%)
    pallas_call x1, Pallas kernels, local(): pl.pallas_call(functools.partial(kernel, nz), out_shape=(jax.ShapeDtypeSt...  90.6 us
    unnamed x3, local copies, waits for them, and re-layouts  2.11 us

profile of v6, /device:TPU:24, one launch (start us, length us, event | category | flops | bytes accessed | tf_op | source)
XLA Modules:
  0.0 95.3 jit_solution(15739537992610558638)
XLA Ops:
  2.6 90.6 %cross_attention.1 = (bf16[1,128,1024]{2,1,0:T(8,128)(2,1)S(1)}, bf16[1,128,1024]{2,1,0:T(8,128)(2,1)S(1)}, f32[256,256]{1,0:T(8,128)S(1)}) custom-call(bf16[1,128,1024]{2,1,0:T(8,128)(2,1)} %queries.1, bf16[1,1,128,1024]{3,2,1,0:T(8,128)(2,1)} %features.1, bf16[8192,256]{1,0:T(8,128)(2,1)} %kv_weight.1, f32[1]{0:T(128)S(6)} %copy.13.gate, ...), custom_call_target="tpu_custom_call" | custom-call | tf_op jit(solution)/shard_map/cross_attention/pallas_call | solution.py:563
  93.1 0.7 copy.16
  93.8 0.7 copy.17
  94.5 0.7 copy.18
